TPU v7x, 32 devices: a whole 2x2x4 slice. The times are simulated.
32 devices in a mesh: ctx: 4 (over y, x), grp: 4 (over z), side: 2 (over core).
Axes of the slice: x: 2, y: 2, z: 4, core: 2. Of those that a mesh axis runs over, the one named last changes fastest.
Arguments:
- tokens: bfloat16 [512, 2048], P(('ctx', 'grp', 'side')), may hold values from -6 to 6
- norm_gain: float32 [2048], replicated, may hold values from 0.25 to 1.75
- combine: float32 [512, 8], P(('ctx', 'grp', 'side')), may hold values from 0.05 to 0.6
- expert_ids: int32 [512, 8], P(('ctx', 'grp', 'side')), may hold values from 0 to 15, all different within a row; in each aligned block of 16 rows (0 to 15, 16 to 31, ...) at most 11 rows name the same one
- w_gate: bfloat16 [16, 2048, 768], P(('ctx', 'grp'), None, 'side'), may hold values from -0.125 to 0.125
- w_up: bfloat16 [16, 2048, 768], P(('ctx', 'grp'), None, 'side'), may hold values from -0.125 to 0.125
- w_down: bfloat16 [16, 768, 2048], P(('ctx', 'grp'), 'side'), may hold values from -0.21875 to 0.21875
- d_out: bfloat16 [512, 2048], P(('ctx', 'grp', 'side')), may hold values from -6 to 6
Outputs:
- mixed: bfloat16 [512, 2048], P(('ctx', 'grp', 'side'))
- d_tokens: bfloat16 [512, 2048], P(('ctx', 'grp', 'side'))
- d_gain: float32 [2048], replicated
- d_combine: float32 [512, 8], P(('ctx', 'grp', 'side'))
- d_w_gate: bfloat16 [16, 2048, 768], P(('ctx', 'grp'), None, 'side')
- d_w_up: bfloat16 [16, 2048, 768], P(('ctx', 'grp'), None, 'side')
- d_w_down: bfloat16 [16, 768, 2048], P(('ctx', 'grp'), 'side')
Inputs may be any that keep to these rules, and one draw needn't show every extreme that they name: `expert_ids`: each row names 8 different experts; among the 16 rows of one device no expert is named more than 11 times, and that bound is reached.
All inputs are finite; a program needn't handle non-finite values.
Results may differ from a plain program's by a relative error of at most 0.0072.
Values may be sent and summed in bfloat16 or wider, within the bound.
A program may use at most 128 MiB of HBM per device.

v0:
```python
import jax
import jax.numpy as jnp
from jax import lax
from jax.sharding import PartitionSpec as P

EPS = 1e-06


def expert_pass(rows, grads, gate_w, up_w, down_w):
    a_gate = jnp.dot(rows, gate_w, preferred_element_type=jnp.float32)
    a_up = jnp.dot(rows, up_w, preferred_element_type=jnp.float32)
    sigmoid_gate = jax.nn.sigmoid(a_gate)
    silu_gate = a_gate * sigmoid_gate
    hidden = (silu_gate * a_up).astype(jnp.bfloat16)
    output = jnp.dot(hidden, down_w, preferred_element_type=jnp.float32)
    d_hidden = lax.dot_general(
        grads, down_w, (((1,), (1,)), ((), ())), preferred_element_type=jnp.float32
    )
    d_up = (d_hidden * silu_gate).astype(jnp.bfloat16)
    d_gate = (d_hidden * a_up * sigmoid_gate * (1.0 + a_gate * (1.0 - sigmoid_gate))).astype(
        jnp.bfloat16
    )
    d_rows = lax.dot_general(
        d_gate, gate_w, (((1,), (1,)), ((), ())), preferred_element_type=jnp.float32
    )
    d_rows = d_rows + lax.dot_general(
        d_up, up_w, (((1,), (1,)), ((), ())), preferred_element_type=jnp.float32
    )
    g_gate = lax.dot_general(
        rows, d_gate, (((0,), (0,)), ((), ())), preferred_element_type=jnp.float32
    )
    g_up = lax.dot_general(rows, d_up, (((0,), (0,)), ((), ())), preferred_element_type=jnp.float32)
    g_down = lax.dot_general(
        hidden, grads, (((0,), (0,)), ((), ())), preferred_element_type=jnp.float32
    )
    return (output, d_rows, g_gate, g_up, g_down)


def local(tokens, norm_gain, combine, expert_ids, w_gate, w_up, w_down, d_out):
    count = tokens.shape[0]
    width = tokens.shape[1]
    chosen = expert_ids.shape[1]
    n_ctx = lax.axis_size("ctx")
    n_grp = lax.axis_size("grp")
    experts = n_ctx * n_grp
    slots = max(2, (4 * count * chosen + 3 * experts - 1) // (3 * experts))
    places = experts * slots
    x_float = tokens.astype(jnp.float32)
    inv_rms = lax.rsqrt(jnp.mean(x_float * x_float, axis=1, keepdims=True) + EPS)
    normed = (x_float * inv_rms * norm_gain).astype(jnp.bfloat16)
    grad_float = d_out.astype(jnp.float32)
    flat_ids = expert_ids.reshape(-1)
    onehot = (flat_ids[:, None] == jnp.arange(experts, dtype=jnp.int32)[None, :]).astype(jnp.int32)
    before = jnp.cumsum(onehot, axis=0) - onehot
    slot = jnp.sum(before * onehot, axis=1)
    target = flat_ids * slots + slot
    select = (target[:, None] == jnp.arange(places, dtype=jnp.int32)[None, :]).astype(jnp.float32)
    per_token = select.reshape(count, chosen, places)
    token_map = jnp.sum(per_token, axis=1).astype(jnp.bfloat16)
    weighted = jnp.sum(per_token * combine[:, :, None], axis=1)
    send_rows = lax.dot_general(
        token_map, normed, (((0,), (0,)), ((), ())), preferred_element_type=jnp.float32
    ).astype(jnp.bfloat16)
    send_grads = lax.dot_general(
        weighted,
        grad_float,
        (((0,), (0,)), ((), ())),
        precision=lax.Precision.HIGHEST,
        preferred_element_type=jnp.float32,
    ).astype(jnp.bfloat16)
    rows_in, grads_in = (
        lax.all_to_all(
            send_rows.reshape(experts, slots, width),
            ("ctx", "grp"),
            split_axis=0,
            concat_axis=0,
            tiled=True,
        ),
        lax.all_to_all(
            send_grads.reshape(experts, slots, width),
            ("ctx", "grp"),
            split_axis=0,
            concat_axis=0,
            tiled=True,
        ),
    )
    full_gate, full_up, full_down = (
        lax.all_gather(w_gate[0], "side", axis=1, tiled=True),
        lax.all_gather(w_up[0], "side", axis=1, tiled=True),
        lax.all_gather(w_down[0], "side", axis=0, tiled=True),
    )
    output, d_rows, g_gate, g_up, g_down = expert_pass(
        rows_in.reshape(places, width),
        grads_in.reshape(places, width),
        full_gate,
        full_up,
        full_down,
    )
    own_gate, own_up, own_down = (
        lax.psum_scatter(g_gate, "side", scatter_dimension=1, tiled=True),
        lax.psum_scatter(g_up, "side", scatter_dimension=1, tiled=True),
        lax.psum_scatter(g_down, "side", scatter_dimension=0, tiled=True),
    )
    back_out = output.astype(jnp.bfloat16)
    back_rows = d_rows.astype(jnp.bfloat16)
    came_out, came_rows = (
        lax.all_to_all(
            back_out.reshape(experts, slots, width),
            ("ctx", "grp"),
            split_axis=0,
            concat_axis=0,
            tiled=True,
        ),
        lax.all_to_all(
            back_rows.reshape(experts, slots, width),
            ("ctx", "grp"),
            split_axis=0,
            concat_axis=0,
            tiled=True,
        ),
    )
    slot_out = jnp.dot(
        select.astype(jnp.bfloat16),
        came_out.reshape(places, width),
        preferred_element_type=jnp.float32,
    ).reshape(count, chosen, width)
    mixed = (x_float + jnp.sum(combine[:, :, None] * slot_out, axis=1)).astype(jnp.bfloat16)
    d_combine = jnp.einsum("tkd,td->tk", slot_out, grad_float, precision=lax.Precision.HIGHEST)
    d_normed = jnp.dot(
        token_map, came_rows.reshape(places, width), preferred_element_type=jnp.float32
    )
    d_gain = lax.psum(jnp.sum(d_normed * x_float * inv_rms, axis=0), ("ctx", "grp", "side"))
    scaled = d_normed * norm_gain
    d_tokens = (
        grad_float
        + inv_rms * scaled
        - x_float * inv_rms**3 * jnp.mean(scaled * x_float, axis=1, keepdims=True)
    )
    return (
        mixed,
        d_tokens.astype(jnp.bfloat16),
        d_gain,
        d_combine,
        own_gate.astype(jnp.bfloat16)[None],
        own_up.astype(jnp.bfloat16)[None],
        own_down.astype(jnp.bfloat16)[None],
    )


def solution(mesh):
    in_specs = (
        P(("ctx", "grp", "side"), None),
        P(),
        P(("ctx", "grp", "side"), None),
        P(("ctx", "grp", "side"), None),
        P(("ctx", "grp"), None, "side"),
        P(("ctx", "grp"), None, "side"),
        P(("ctx", "grp"), "side", None),
        P(("ctx", "grp", "side"), None),
    )
    out_specs = (
        P(("ctx", "grp", "side"), None),
        P(("ctx", "grp", "side"), None),
        P(),
        P(("ctx", "grp", "side"), None),
        P(("ctx", "grp"), None, "side"),
        P(("ctx", "grp"), None, "side"),
        P(("ctx", "grp"), "side", None),
    )
    return jax.shard_map(local, mesh=mesh, in_specs=in_specs, out_specs=out_specs, check_vma=False)
```

profile of v0, /device:TPU:12, one launch (start us, length us, event | category | flops | bytes accessed | tf_op | source)
XLA Modules:
  0.0 222.5 jit_solution(12201147010498002594)
XLA Ops:
  7.2 0.7 all-gather.11.cloned.1.call-update
  8.0 0.7 all-gather.9.cloned.1.call-update
  8.7 0.1 copy.23
  8.8 0.1 eq.49
  8.9 0.1 fusion.41
  9.0 0.2 reduce_window_sum.11
  9.2 0.2 select_reduce_fusion.1
  9.4 0.1 reduce_sum.66
  9.5 0.2 select_reduce_fusion
  9.7 0.8 convolution_convert_fusion
  10.5 1.2 reshape.111
  11.7 7.2 %all-to-all-start.2 = ((bf16[16,11,2048]{2,1,0:T(8,128)(2,1)}), bf16[16,11,2048]{2,1,0:T(8,128)(2,1)S(1)}, u32[]{:S(2)}, u32[]{:S(2)}) async-start(bf16[16,11,2048]{2,1,0:T(8,128)(2,1)} %reshape.111), calls=%async_computation.2 | async-start | bytes 2097152 | tf_op jit(solution)/shard_map/all_to_all | solution.py:79
  18.9 0.7 all-gather.7.cloned.1.call-update
  19.6 0.1 fusion.22
  19.8 0.5 multiply_multiply_fusion
  20.3 0.4 convolution_convert_fusion.1
  20.7 1.2 reshape.107
  21.9 20.6 %all-to-all-done.2 = bf16[16,11,2048]{2,1,0:T(8,128)(2,1)S(1)} async-done(((bf16[16,11,2048]{2,1,0:T(8,128)(2,1)}), bf16[16,11,2048]{2,1,0:T(8,128)(2,1)S(1)}, u32[]{:S(2)}, u32[]{:S(2)}) %all-to-all-start.2) | async-done | bytes 720928 | tf_op jit(solution)/shard_map/all_to_all | solution.py:79
  42.5 7.5 %all-to-all-start = ((bf16[16,11,2048]{2,1,0:T(8,128)(2,1)}), bf16[16,11,2048]{2,1,0:T(8,128)(2,1)S(1)}, u32[]{:S(2)}, u32[]{:S(2)}) async-start(bf16[16,11,2048]{2,1,0:T(8,128)(2,1)} %reshape.107), calls=%async_computation | async-start | bytes 2097152 | tf_op jit(solution)/shard_map/all_to_all | solution.py:72
  50.0 0.3 reshape.112
  50.3 22.6 %all-to-all-done = bf16[16,11,2048]{2,1,0:T(8,128)(2,1)S(1)} async-done(((bf16[16,11,2048]{2,1,0:T(8,128)(2,1)}), bf16[16,11,2048]{2,1,0:T(8,128)(2,1)S(1)}, u32[]{:S(2)}, u32[]{:S(2)}) %all-to-all-start) | async-done | bytes 720928 | tf_op jit(solution)/shard_map/all_to_all | solution.py:72
  72.9 0.3 reshape.108
  73.2 3.1 %fusion = f32[176,768]{1,0:T(8,128)S(1)} fusion(bf16[176,2048]{1,0:T(8,128)(2,1)S(1)} %reshape.112, bf16[1,768,2048]{2,1,0:T(8,128)(2,1)} %all-gather.11.cloned.1.call-done), kind=kOutput, calls=%fused_computation | convolution fusion | flops 553648128 | bytes 4407296 | tf_op jit(solution)/shard_map/dot_general | solution.py:16
  76.4 2.6 %fusion.6 = f32[176,768]{1,0:T(8,128)S(1)} fusion(bf16[176,2048]{1,0:T(8,128)(2,1)S(1)} %reshape.108, bf16[1,2048,768]{2,1,0:T(8,128)(2,1)} %all-gather.9.cloned.1.call-done), kind=kOutput, calls=%fused_computation.6 | convolution fusion | flops 553648128 | bytes 4407296 | tf_op jit(solution)/shard_map/dot_general | solution.py:11
  79.0 2.8 %multiply_convert_fusion.1 = (bf16[176,768]{1,0:T(8,128)(2,1)S(1)}, bf16[176,768]{1,0:T(8,128)(2,1)S(1)}, bf16[176,768]{1,0:T(8,128)(2,1)S(1)}) fusion(f32[176,768]{1,0:T(8,128)S(1)} %fusion, f32[176,768]{1,0:T(8,128)S(1)} %fusion.6, bf16[176,2048]{1,0:T(8,128)(2,1)S(1)} %reshape.108, bf16[1,2048,768]{2,1,0:T(8,128)(2,1)} %all-gather.7.cloned.1.call-done), kind=kOutput, calls=%fused_computation.22 | convolution fusion | flops 555675648 | bytes 5758976 | tf_op jit(solution)/shard_map/dot_general | solution.py:10
  81.8 3.6 %fusion.47 = f32[768,2048]{1,0:T(8,128)} fusion(bf16[176,768]{1,0:T(8,128)(2,1)S(1)} %get-tuple-element.13, bf16[176,2048]{1,0:T(8,128)(2,1)S(1)} %reshape.112), kind=kOutput, calls=%fused_computation.66 | convolution fusion | flops 553648128 | bytes 7282688 | tf_op jit(solution)/shard_map/dot_general | solution.py:33
  85.5 3.7 %fusion.45 = f32[2048,768]{1,0:T(8,128)} fusion(bf16[176,2048]{1,0:T(8,128)(2,1)S(1)} %reshape.108, bf16[176,768]{1,0:T(8,128)(2,1)S(1)} %get-tuple-element.11), kind=kOutput, calls=%fused_computation.64 | convolution fusion | flops 553648128 | bytes 7282688 | tf_op jit(solution)/shard_map/dot_general | solution.py:29
  89.3 4.0 %fusion.46 = f32[2048,768]{1,0:T(8,128)} fusion(bf16[176,2048]{1,0:T(8,128)(2,1)S(1)} %reshape.108, bf16[176,768]{1,0:T(8,128)(2,1)S(1)} %get-tuple-element.12), kind=kOutput, calls=%fused_computation.65 | convolution fusion | flops 553648128 | bytes 7282688 | tf_op jit(solution)/shard_map/dot_general | solution.py:32
  93.4 3.7 %fusion.15 = bf16[176,2048]{1,0:T(8,128)(2,1)} fusion(bf16[176,768]{1,0:T(8,128)(2,1)S(1)} %get-tuple-element.13, bf16[1,768,2048]{2,1,0:T(8,128)(2,1)} %all-gather.11.cloned.1.call-done), kind=kOutput, calls=%fused_computation.13 | convolution fusion | flops 554008576 | bytes 4136960 | tf_op jit(solution)/shard_map/dot_general | solution.py:15
  97.1 2.6 %reshape.109 = bf16[16,11,2048]{2,1,0:T(8,128)(2,1)} reshape(bf16[176,2048]{1,0:T(8,128)(2,1)} %fusion.15) | data formatting | bytes 1441792 | tf_op jit(solution)/shard_map/reshape | solution.py:108
  99.6 9.3 %all-to-all-start.1 = ((bf16[16,11,2048]{2,1,0:T(8,128)(2,1)}), bf16[16,11,2048]{2,1,0:T(8,128)(2,1)}, u32[]{:S(2)}, u32[]{:S(2)}) async-start(bf16[16,11,2048]{2,1,0:T(8,128)(2,1)} %reshape.109), calls=%async_computation.1 | async-start | bytes 2097152 | tf_op jit(solution)/shard_map/all_to_all | solution.py:107
  108.9 2.3 %fusion.4 = f32[176,2048]{1,0:T(8,128)S(1)} fusion(bf16[176,768]{1,0:T(8,128)(2,1)} %copy-done.4, bf16[1,2048,768]{2,1,0:T(8,128)(2,1)S(1)} %copy-done), kind=kOutput, calls=%fused_computation.4 | convolution fusion | flops 553648128 | bytes 4857856 | tf_op jit(solution)/shard_map/dot_general | solution.py:26
  111.2 1.2 fusion.18
  112.4 1.2 reshape.113
  113.7 17.7 %all-to-all-done.1 = bf16[16,11,2048]{2,1,0:T(8,128)(2,1)} async-done(((bf16[16,11,2048]{2,1,0:T(8,128)(2,1)}), bf16[16,11,2048]{2,1,0:T(8,128)(2,1)}, u32[]{:S(2)}, u32[]{:S(2)}) %all-to-all-start.1) | async-done | bytes 720928 | tf_op jit(solution)/shard_map/all_to_all | solution.py:107
  131.4 7.5 %all-to-all-start.3 = ((bf16[16,11,2048]{2,1,0:T(8,128)(2,1)}), bf16[16,11,2048]{2,1,0:T(8,128)(2,1)S(1)}, u32[]{:S(2)}, u32[]{:S(2)}) async-start(bf16[16,11,2048]{2,1,0:T(8,128)(2,1)} %reshape.113), calls=%async_computation.3 | async-start | bytes 2097152 | tf_op jit(solution)/shard_map/all_to_all | solution.py:114
  138.9 1.5 reshape.118
  140.4 0.5 multiply_reduce_fusion
  140.9 1.1 fusion.32
  142.1 0.7 copy.28
  142.8 19.0 %all-to-all-done.3 = bf16[16,11,2048]{2,1,0:T(8,128)(2,1)S(1)} async-done(((bf16[16,11,2048]{2,1,0:T(8,128)(2,1)}), bf16[16,11,2048]{2,1,0:T(8,128)(2,1)S(1)}, u32[]{:S(2)}, u32[]{:S(2)}) %all-to-all-start.3) | async-done | bytes 720928 | tf_op jit(solution)/shard_map/all_to_all | solution.py:114
  161.8 0.3 reshape.114
  162.1 0.3 fusion.31
  162.4 42.8 %psum.7 = f32[2048]{0:T(1024)} all-reduce(f32[2048]{0:T(1024)S(1)} %get-tuple-element.7), channel_id=1, replica_groups=mesh['ctx'=4,'grp'=4,'side'=2] {'ctx','grp','side'}, use_global_device_ids=true, to_apply=%region_8.9 | all-reduce | flops 2048 | bytes 16384 | tf_op jit(solution)/shard_map/psum | solution.py:132
  205.2 0.7 fusion.28
  206.0 3.3 %convert_bitcast_fusion = bf16[1,384,2048]{2,1,0:T(8,128)(2,1)} fusion(f32[384,2048]{1,0:T(8,128)} %reduce-scatter.8.cloned.1.call-done), kind=kLoop, calls=%fused_computation.17 | loop fusion | flops 786432 | bytes 4718592 | tf_op jit(solution)/shard_map/broadcast_in_dim | solution.py:146
  209.2 3.2 %convert_bitcast_fusion.2 = bf16[1,2048,384]{2,1,0:T(8,128)(2,1)} fusion(f32[2048,384]{1,0:T(8,128)} %reduce-scatter.4.cloned.1.call-done), kind=kLoop, calls=%fused_computation.19 | loop fusion | flops 786432 | bytes 4718592 | tf_op jit(solution)/shard_map/broadcast_in_dim | solution.py:144
  212.4 3.2 %convert_bitcast_fusion.1 = bf16[1,2048,384]{2,1,0:T(8,128)(2,1)} fusion(f32[2048,384]{1,0:T(8,128)} %reduce-scatter.6.cloned.1.call-done), kind=kLoop, calls=%fused_computation.18 | loop fusion | flops 786432 | bytes 4718592 | tf_op jit(solution)/shard_map/broadcast_in_dim | solution.py:145
  (56 shorter events, 0.5 us)
Async XLA Ops:
  7.2 1.5 copy-start.16
  7.2 1.6 copy-start.17
  7.2 2.5 %copy-start.5 = (bf16[16,2048]{1,0:T(8,128)(2,1)S(1)}, bf16[16,2048]{1,0:T(8,128)(2,1)}, u32[]{:S(2)}) copy-start(bf16[16,2048]{1,0:T(8,128)(2,1)} %param.15) | copy-start | bytes 196612
  7.2 66.0 %all-gather.11.cloned.1.call-start = ((), (), s32[]{:S(2)}) async-start(), calls=%async_computation.12 | async-start | bytes 4718592 | tf_op jit(solution)/shard_map/all_gather | solution.py:90
  7.9 68.4 %all-gather.9.cloned.1.call-start = ((), (), s32[]{:S(2)}) async-start(), calls=%async_computation.11 | async-start | bytes 4718592 | tf_op jit(solution)/shard_map/all_gather | solution.py:89
  8.8 10.8 %copy-start.12 = (f32[16,8]{1,0:T(8,128)}, f32[16,8]{1,0:T(8,128)S(1)}, u32[]{:S(2)}) copy-start(f32[16,8]{1,0:T(8,128)S(1)} %copy.23) | copy-start | bytes 1540
  9.5 10.3 %copy-start.10 = (s32[16,8]{1,0:T(8,128)}, s32[16,8]{1,0:T(8,128)S(1)}, u32[]{:S(2)}) copy-start(s32[16,8]{1,0:T(8,128)S(1)} %multiply_add_fusion) | copy-start | bytes 1540
  9.5 10.1 %copy-start.6 = (bf16[16,2048]{1,0:T(8,128)(2,1)S(1)}, bf16[16,2048]{1,0:T(8,128)(2,1)}, u32[]{:S(2)}) copy-start(bf16[16,2048]{1,0:T(8,128)(2,1)} %param.8) | copy-start | bytes 196612
  9.7 10.6 %copy-start.8 = (bf16[16,176]{1,0:T(8,128)(2,1)}, bf16[16,176]{1,0:T(8,128)(2,1)S(1)}, u32[]{:S(2)}) copy-start(bf16[16,176]{1,0:T(8,128)(2,1)S(1)} %get-tuple-element.10) | copy-start | bytes 16900
  9.7 10.6 %copy-start.7 = (f32[2048]{0:T(1024)S(1)}, f32[2048]{0:T(1024)}, u32[]{:S(2)}) copy-start(f32[2048]{0:T(1024)} %param.9) | copy-start | bytes 24580
  11.7 30.8 %all-to-all-start.2 = ((bf16[16,11,2048]{2,1,0:T(8,128)(2,1)}), bf16[16,11,2048]{2,1,0:T(8,128)(2,1)S(1)}, u32[]{:S(2)}, u32[]{:S(2)}) async-start(bf16[16,11,2048]{2,1,0:T(8,128)(2,1)} %reshape.111), calls=%async_computation.2 | async-start | bytes 2097152 | tf_op jit(solution)/shard_map/all_to_all | solution.py:79
  18.9 60.1 %all-gather.7.cloned.1.call-start = ((), (), s32[]{:S(2)}) async-start(), calls=%async_computation.10 | async-start | bytes 4718592 | tf_op jit(solution)/shard_map/all_gather | solution.py:88
  20.3 22.2 %copy-start.14 = (f32[16]{0:T(128)}, f32[16]{0:T(128)S(1)}, u32[]{:S(2)}) copy-start(f32[16]{0:T(128)S(1)} %get-tuple-element.17) | copy-start | bytes 196
  42.5 30.5 %all-to-all-start = ((bf16[16,11,2048]{2,1,0:T(8,128)(2,1)}), bf16[16,11,2048]{2,1,0:T(8,128)(2,1)S(1)}, u32[]{:S(2)}, u32[]{:S(2)}) async-start(bf16[16,11,2048]{2,1,0:T(8,128)(2,1)} %reshape.107), calls=%async_computation | async-start | bytes 2097152 | tf_op jit(solution)/shard_map/all_to_all | solution.py:72
  49.9 156.0 %reduce-scatter.8.cloned.1.call-start = ((), (), s32[]{:S(2)}) async-start(), calls=%async_computation.9 | async-start | bytes 9437184 | tf_op jit(solution)/shard_map/reduce_scatter | solution.py:102
  81.8 3.7 %copy-start.2 = (bf16[176,768]{1,0:T(8,128)(2,1)}, bf16[176,768]{1,0:T(8,128)(2,1)S(1)}, u32[]{:S(2)}) copy-start(bf16[176,768]{1,0:T(8,128)(2,1)S(1)} %get-tuple-element.11) | copy-start | bytes 811012
  81.8 7.5 %copy-start.4 = (bf16[176,768]{1,0:T(8,128)(2,1)}, bf16[176,768]{1,0:T(8,128)(2,1)S(1)}, u32[]{:S(2)}) copy-start(bf16[176,768]{1,0:T(8,128)(2,1)S(1)} %get-tuple-element.12) | copy-start | bytes 811012
  85.5 123.8 %reduce-scatter.4.cloned.1.call-start = ((), (), s32[]{:S(2)}) async-start(), calls=%async_computation.7 | async-start | bytes 9437184 | tf_op jit(solution)/shard_map/reduce_scatter | solution.py:100
  89.3 123.2 %reduce-scatter.6.cloned.1.call-start = ((), (), s32[]{:S(2)}) async-start(), calls=%async_computation.8 | async-start | bytes 9437184 | tf_op jit(solution)/shard_map/reduce_scatter | solution.py:101
  93.3 15.6 %copy-start = (bf16[1,2048,768]{2,1,0:T(8,128)(2,1)S(1)}, bf16[1,2048,768]{2,1,0:T(8,128)(2,1)}, u32[]{:S(2)}) copy-start(bf16[1,2048,768]{2,1,0:T(8,128)(2,1)} %all-gather.9.cloned.1.call-done) | copy-start | bytes 9437188
  99.6 11.6 %copy-start.3 = (bf16[176,768]{1,0:T(8,128)(2,1)S(1)}, bf16[176,768]{1,0:T(8,128)(2,1)}, u32[]{:S(2)}) copy-start(bf16[176,768]{1,0:T(8,128)(2,1)} %copy-done.2) | copy-start | bytes 811012
  99.6 31.8 %all-to-all-start.1 = ((bf16[16,11,2048]{2,1,0:T(8,128)(2,1)}), bf16[16,11,2048]{2,1,0:T(8,128)(2,1)}, u32[]{:S(2)}, u32[]{:S(2)}) async-start(bf16[16,11,2048]{2,1,0:T(8,128)(2,1)} %reshape.109), calls=%async_computation.1 | async-start | bytes 2097152 | tf_op jit(solution)/shard_map/all_to_all | solution.py:107
  108.9 2.3 %copy-start.1 = (bf16[1,2048,768]{2,1,0:T(8,128)(2,1)S(1)}, bf16[1,2048,768]{2,1,0:T(8,128)(2,1)}, u32[]{:S(2)}) copy-start(bf16[1,2048,768]{2,1,0:T(8,128)(2,1)} %all-gather.7.cloned.1.call-done) | copy-start | bytes 9437188
  112.4 28.0 %copy-start.11 = (s32[16,8]{1,0:T(8,128)S(1)}, s32[16,8]{1,0:T(8,128)}, u32[]{:S(2)}) copy-start(s32[16,8]{1,0:T(8,128)} %copy-done.10) | copy-start | bytes 1540
  112.4 28.0 %copy-start.13 = (f32[16,8]{1,0:T(8,128)S(1)}, f32[16,8]{1,0:T(8,128)}, u32[]{:S(2)}) copy-start(f32[16,8]{1,0:T(8,128)} %copy-done.12) | copy-start | bytes 1540
  131.4 30.4 %all-to-all-start.3 = ((bf16[16,11,2048]{2,1,0:T(8,128)(2,1)}), bf16[16,11,2048]{2,1,0:T(8,128)(2,1)S(1)}, u32[]{:S(2)}, u32[]{:S(2)}) async-start(bf16[16,11,2048]{2,1,0:T(8,128)(2,1)} %reshape.113), calls=%async_computation.3 | async-start | bytes 2097152 | tf_op jit(solution)/shard_map/all_to_all | solution.py:114
  138.9 23.2 %copy-start.9 = (bf16[16,176]{1,0:T(8,128)(2,1)S(1)}, bf16[16,176]{1,0:T(8,128)(2,1)}, u32[]{:S(2)}) copy-start(bf16[16,176]{1,0:T(8,128)(2,1)} %copy-done.8) | copy-start | bytes 16900
  138.9 23.2 %copy-start.15 = (f32[16]{0:T(128)S(1)}, f32[16]{0:T(128)}, u32[]{:S(2)}) copy-start(f32[16]{0:T(128)} %copy-done.14) | copy-start | bytes 196
  140.4 64.8 %copy-start.18 = (f32[16]{0:T(128)S(1)}, f32[16]{0:T(128)}, u32[]{:S(2)}) copy-start(f32[16]{0:T(128)} %get-tuple-element.16) | copy-start | bytes 196
Sparse Core Ops, SparseCore 0:
  9.6 13.4 all-gather.10
  24.6 13.1 all-gather.8
  39.4 13.1 all-gather.6
  85.6 15.8 reduce-scatter.7
  103.6 15.1 reduce-scatter.3
  120.9 15.0 reduce-scatter.5
where the time goes:
time: 223 us; the launch traced here: 222 us
  waiting for transfers between devices  82.1 us (37%)
  blocking collectives  42.8 us (19%)
  starting transfers between devices  31.6 us (14%)
  matrix products  30.1 us (13%)
  between operations  14.5 us (7%)
  other arithmetic  11.7 us (5%)
  local copies, waits for them, and re-layouts  9.69 us (4%)
    psum x1, blocking collectives, local(): lax.psum(jnp.sum(d_normed * x_float * inv_rms, axis=0), ('ctx', 'grp', 's...  42.8 us
    all_to_all x1, waiting for transfers between devices, local(): lax.all_to_all(send_rows.reshape(experts, slots, width), ('ctx', 'grp'),...  22.6 us
    all_to_all x1, waiting for transfers between devices, local(): lax.all_to_all(send_grads.reshape(experts, slots, width), ('ctx', 'grp'),...  20.6 us
    all_to_all x1, waiting for transfers between devices, local(): lax.all_to_all(back_rows.reshape(experts, slots, width), ('ctx', 'grp'),...  19 us
    all_to_all x1, waiting for transfers between devices, local(): lax.all_to_all(back_out.reshape(experts, slots, width), ('ctx', 'grp'), s...  17.7 us
    all_to_all x1, starting transfers between devices, local(): lax.all_to_all(back_out.reshape(experts, slots, width), ('ctx', 'grp'), s...  9.28 us
    all_to_all x1, starting transfers between devices, local(): lax.all_to_all(back_rows.reshape(experts, slots, width), ('ctx', 'grp'),...  7.49 us
    all_to_all x1, starting transfers between devices, local(): lax.all_to_all(send_rows.reshape(experts, slots, width), ('ctx', 'grp'),...  7.48 us
  transfers between devices with their start and end apart: 10, of which 4 were waited for; matrix products, arithmetic and copies ran while one was open for 19% of the time, Pallas kernels for 0%

commit v1 on v0

--- a/solution.py
+++ b/solution.py
@@ -129,7 +129,9 @@
     d_normed = jnp.dot(
         token_map, came_rows.reshape(places, width), preferred_element_type=jnp.float32
     )
-    d_gain = lax.psum(jnp.sum(d_normed * x_float * inv_rms, axis=0), ("ctx", "grp", "side"))
+    d_gain = lax.psum(
+        lax.psum(jnp.sum(d_normed * x_float * inv_rms, axis=0), "ctx"), ("grp", "side")
+    )
     scaled = d_normed * norm_gain
     d_tokens = (
         grad_float

time: 223 us -> 208 us (0.933)
  the two profiles are of different devices: /device:TPU:12 before, /device:TPU:0 now
where the time goes in v1:
time: 208 us; the launch traced here: 207 us
  waiting for transfers between devices  97.1 us (47%)
  matrix products  31.4 us (15%)
  blocking collectives  22.7 us (11%)
  starting transfers between devices  20.6 us (10%)
  between operations  14.5 us (7%)
  other arithmetic  11.7 us (6%)
  local copies, waits for them, and re-layouts  9.45 us (5%)
    all_to_all x1, waiting for transfers between devices, local(): lax.all_to_all(send_rows.reshape(experts, slots, width), ('ctx', 'grp'),...  26.4 us
    all_to_all x1, waiting for transfers between devices, local(): lax.all_to_all(send_grads.reshape(experts, slots, width), ('ctx', 'grp'),...  24.4 us
    all_to_all x1, waiting for transfers between devices, local(): lax.all_to_all(back_rows.reshape(experts, slots, width), ('ctx', 'grp'),...  22.6 us
    all_to_all x1, waiting for transfers between devices, local(): lax.all_to_all(back_out.reshape(experts, slots, width), ('ctx', 'grp'), s...  21.5 us
    psum x1, blocking collectives, local(): lax.psum(lax.psum(jnp.sum(d_normed * x_float * inv_rms, axis=0), 'ctx'),...  14.5 us
    all_to_all x1, starting transfers between devices, local(): lax.all_to_all(send_grads.reshape(experts, slots, width), ('ctx', 'grp'),...  8.34 us
    psum x1, blocking collectives, local(): lax.psum(jnp.sum(d_normed * x_float * inv_rms, axis=0), 'ctx')  8.15 us
    dot_general x1, matrix products, expert_pass(): lax.dot_general(rows, d_up, (((0,), (0,)), ((), ())), preferred_element_t...  4.81 us
  transfers between devices with their start and end apart: 10, of which 4 were waited for; matrix products, arithmetic and copies ran while one was open for 21% of the time, Pallas kernels for 0%

profile of v1, /device:TPU:0, one launch (start us, length us, event | category | flops | bytes accessed | tf_op | source)
XLA Modules:
  0.0 207.3 jit_solution(8917621593842196652)
XLA Ops:
  7.2 0.7 all-gather.11.cloned.1.call-update
  8.0 0.7 all-gather.9.cloned.1.call-update
  8.8 0.1 eq.49
  8.9 0.1 fusion.41
  9.0 0.2 reduce_window_sum.11
  9.2 0.2 select_reduce_fusion.1
  9.4 0.1 reduce_sum.66
  9.5 0.2 select_reduce_fusion
  9.7 0.8 convolution_convert_fusion
  10.5 1.2 reshape.111
  11.7 8.3 %all-to-all-start.2 = ((bf16[16,11,2048]{2,1,0:T(8,128)(2,1)}), bf16[16,11,2048]{2,1,0:T(8,128)(2,1)S(1)}, u32[]{:S(2)}, u32[]{:S(2)}) async-start(bf16[16,11,2048]{2,1,0:T(8,128)(2,1)} %reshape.111), calls=%async_computation.2 | async-start | bytes 2097152 | tf_op jit(solution)/shard_map/all_to_all | solution.py:79
  20.1 0.7 all-gather.7.cloned.1.call-update
  20.8 0.1 fusion.22
  20.9 0.6 multiply_multiply_fusion
  21.5 0.4 convolution_convert_fusion.1
  21.9 1.2 reshape.107
  23.2 24.4 %all-to-all-done.2 = bf16[16,11,2048]{2,1,0:T(8,128)(2,1)S(1)} async-done(((bf16[16,11,2048]{2,1,0:T(8,128)(2,1)}), bf16[16,11,2048]{2,1,0:T(8,128)(2,1)S(1)}, u32[]{:S(2)}, u32[]{:S(2)}) %all-to-all-start.2) | async-done | bytes 720928 | tf_op jit(solution)/shard_map/all_to_all | solution.py:79
  47.5 3.7 %all-to-all-start = ((bf16[16,11,2048]{2,1,0:T(8,128)(2,1)}), bf16[16,11,2048]{2,1,0:T(8,128)(2,1)S(1)}, u32[]{:S(2)}, u32[]{:S(2)}) async-start(bf16[16,11,2048]{2,1,0:T(8,128)(2,1)} %reshape.107), calls=%async_computation | async-start | bytes 2097152 | tf_op jit(solution)/shard_map/all_to_all | solution.py:72
  51.2 0.3 reshape.112
  51.5 26.4 %all-to-all-done = bf16[16,11,2048]{2,1,0:T(8,128)(2,1)S(1)} async-done(((bf16[16,11,2048]{2,1,0:T(8,128)(2,1)}), bf16[16,11,2048]{2,1,0:T(8,128)(2,1)S(1)}, u32[]{:S(2)}, u32[]{:S(2)}) %all-to-all-start) | async-done | bytes 720928 | tf_op jit(solution)/shard_map/all_to_all | solution.py:72
  78.0 0.3 reshape.108
  78.3 3.1 %fusion = f32[176,768]{1,0:T(8,128)S(1)} fusion(bf16[176,2048]{1,0:T(8,128)(2,1)S(1)} %reshape.112, bf16[1,768,2048]{2,1,0:T(8,128)(2,1)} %all-gather.11.cloned.1.call-done), kind=kOutput, calls=%fused_computation | convolution fusion | flops 553648128 | bytes 4407296 | tf_op jit(solution)/shard_map/dot_general | solution.py:16
  81.4 2.6 %fusion.6 = f32[176,768]{1,0:T(8,128)S(1)} fusion(bf16[176,2048]{1,0:T(8,128)(2,1)S(1)} %reshape.108, bf16[1,2048,768]{2,1,0:T(8,128)(2,1)} %all-gather.9.cloned.1.call-done), kind=kOutput, calls=%fused_computation.6 | convolution fusion | flops 553648128 | bytes 4407296 | tf_op jit(solution)/shard_map/dot_general | solution.py:11
  84.1 2.8 %multiply_convert_fusion.1 = (bf16[176,768]{1,0:T(8,128)(2,1)S(1)}, bf16[176,768]{1,0:T(8,128)(2,1)S(1)}, bf16[176,768]{1,0:T(8,128)(2,1)S(1)}) fusion(f32[176,768]{1,0:T(8,128)S(1)} %fusion, f32[176,768]{1,0:T(8,128)S(1)} %fusion.6, bf16[176,2048]{1,0:T(8,128)(2,1)S(1)} %reshape.108, bf16[1,2048,768]{2,1,0:T(8,128)(2,1)} %all-gather.7.cloned.1.call-done), kind=kOutput, calls=%fused_computation.22 | convolution fusion | flops 555675648 | bytes 5758976 | tf_op jit(solution)/shard_map/dot_general | solution.py:10
  86.9 3.6 %fusion.47 = f32[768,2048]{1,0:T(8,128)} fusion(bf16[176,768]{1,0:T(8,128)(2,1)S(1)} %get-tuple-element.13, bf16[176,2048]{1,0:T(8,128)(2,1)S(1)} %reshape.112), kind=kOutput, calls=%fused_computation.66 | convolution fusion | flops 553648128 | bytes 7282688 | tf_op jit(solution)/shard_map/dot_general | solution.py:33
  90.6 4.0 %fusion.45 = f32[2048,768]{1,0:T(8,128)} fusion(bf16[176,2048]{1,0:T(8,128)(2,1)S(1)} %reshape.108, bf16[176,768]{1,0:T(8,128)(2,1)S(1)} %get-tuple-element.11), kind=kOutput, calls=%fused_computation.64 | convolution fusion | flops 553648128 | bytes 7282688 | tf_op jit(solution)/shard_map/dot_general | solution.py:29
  94.7 4.8 %fusion.46 = f32[2048,768]{1,0:T(8,128)} fusion(bf16[176,2048]{1,0:T(8,128)(2,1)S(1)} %reshape.108, bf16[176,768]{1,0:T(8,128)(2,1)S(1)} %get-tuple-element.12), kind=kOutput, calls=%fused_computation.65 | convolution fusion | flops 553648128 | bytes 7282688 | tf_op jit(solution)/shard_map/dot_general | solution.py:32
  99.5 3.9 %fusion.15 = bf16[176,2048]{1,0:T(8,128)(2,1)} fusion(bf16[176,768]{1,0:T(8,128)(2,1)S(1)} %get-tuple-element.13, bf16[1,768,2048]{2,1,0:T(8,128)(2,1)} %all-gather.11.cloned.1.call-done), kind=kOutput, calls=%fused_computation.13 | convolution fusion | flops 554008576 | bytes 4136960 | tf_op jit(solution)/shard_map/dot_general | solution.py:15
  103.4 2.3 %reshape.109 = bf16[16,11,2048]{2,1,0:T(8,128)(2,1)} reshape(bf16[176,2048]{1,0:T(8,128)(2,1)} %fusion.15) | data formatting | bytes 1441792 | tf_op jit(solution)/shard_map/reshape | solution.py:108
  105.7 4.5 %all-to-all-start.1 = ((bf16[16,11,2048]{2,1,0:T(8,128)(2,1)}), bf16[16,11,2048]{2,1,0:T(8,128)(2,1)}, u32[]{:S(2)}, u32[]{:S(2)}) async-start(bf16[16,11,2048]{2,1,0:T(8,128)(2,1)} %reshape.109), calls=%async_computation.1 | async-start | bytes 2097152 | tf_op jit(solution)/shard_map/all_to_all | solution.py:107
  110.2 2.3 %fusion.4 = f32[176,2048]{1,0:T(8,128)S(1)} fusion(bf16[176,768]{1,0:T(8,128)(2,1)} %copy-done.4, bf16[1,2048,768]{2,1,0:T(8,128)(2,1)S(1)} %copy-done), kind=kOutput, calls=%fused_computation.4 | convolution fusion | flops 553648128 | bytes 4857856 | tf_op jit(solution)/shard_map/dot_general | solution.py:26
  112.5 1.2 fusion.18
  113.7 1.2 reshape.113
  115.0 21.5 %all-to-all-done.1 = bf16[16,11,2048]{2,1,0:T(8,128)(2,1)} async-done(((bf16[16,11,2048]{2,1,0:T(8,128)(2,1)}), bf16[16,11,2048]{2,1,0:T(8,128)(2,1)}, u32[]{:S(2)}, u32[]{:S(2)}) %all-to-all-start.1) | async-done | bytes 720928 | tf_op jit(solution)/shard_map/all_to_all | solution.py:107
  136.4 3.8 %all-to-all-start.3 = ((bf16[16,11,2048]{2,1,0:T(8,128)(2,1)}), bf16[16,11,2048]{2,1,0:T(8,128)(2,1)S(1)}, u32[]{:S(2)}, u32[]{:S(2)}) async-start(bf16[16,11,2048]{2,1,0:T(8,128)(2,1)} %reshape.113), calls=%async_computation.3 | async-start | bytes 2097152 | tf_op jit(solution)/shard_map/all_to_all | solution.py:114
  140.3 1.5 reshape.118
  141.8 0.5 multiply_reduce_fusion
  142.3 1.1 fusion.32
  143.5 0.7 copy.28
  144.2 22.6 %all-to-all-done.3 = bf16[16,11,2048]{2,1,0:T(8,128)(2,1)S(1)} async-done(((bf16[16,11,2048]{2,1,0:T(8,128)(2,1)}), bf16[16,11,2048]{2,1,0:T(8,128)(2,1)S(1)}, u32[]{:S(2)}, u32[]{:S(2)}) %all-to-all-start.3) | async-done | bytes 720928 | tf_op jit(solution)/shard_map/all_to_all | solution.py:114
  166.8 0.3 reshape.114
  167.1 0.3 fusion.31
  167.4 8.2 %psum.14 = f32[2048]{0:T(1024)S(1)} all-reduce(f32[2048]{0:T(1024)S(1)} %get-tuple-element.7), channel_id=1, replica_groups=mesh['ctx'=4,'grp'=4,'side'=2] {'ctx'}, use_global_device_ids=true, to_apply=%region_8.9 | all-reduce | flops 2048 | bytes 16384 | tf_op jit(solution)/shard_map/psum | solution.py:133
  175.6 14.5 %psum.15 = f32[2048]{0:T(1024)} all-reduce(f32[2048]{0:T(1024)S(1)} %psum.14), channel_id=1, replica_groups=mesh['ctx'=4,'grp'=4,'side'=2] {'grp','side'}, use_global_device_ids=true, to_apply=%region_9.10 | all-reduce | flops 2048 | bytes 16384 | tf_op jit(solution)/shard_map/psum | solution.py:132
  190.1 0.7 fusion.28
  190.8 3.3 %convert_bitcast_fusion = bf16[1,384,2048]{2,1,0:T(8,128)(2,1)} fusion(f32[384,2048]{1,0:T(8,128)} %reduce-scatter.8.cloned.1.call-done), kind=kLoop, calls=%fused_computation.17 | loop fusion | flops 786432 | bytes 4718592 | tf_op jit(solution)/shard_map/broadcast_in_dim | solution.py:148
  194.1 3.2 %convert_bitcast_fusion.2 = bf16[1,2048,384]{2,1,0:T(8,128)(2,1)} fusion(f32[2048,384]{1,0:T(8,128)} %reduce-scatter.4.cloned.1.call-done), kind=kLoop, calls=%fused_computation.19 | loop fusion | flops 786432 | bytes 4718592 | tf_op jit(solution)/shard_map/broadcast_in_dim | solution.py:146
  197.3 3.2 %convert_bitcast_fusion.1 = bf16[1,2048,384]{2,1,0:T(8,128)(2,1)} fusion(f32[2048,384]{1,0:T(8,128)} %reduce-scatter.6.cloned.1.call-done), kind=kLoop, calls=%fused_computation.18 | loop fusion | flops 786432 | bytes 4718592 | tf_op jit(solution)/shard_map/broadcast_in_dim | solution.py:147
  (57 shorter events, 0.6 us)
Async XLA Ops:
  7.2 1.5 copy-start.16
  7.2 1.6 copy-start.17
  7.2 2.5 %copy-start.5 = (bf16[16,2048]{1,0:T(8,128)(2,1)S(1)}, bf16[16,2048]{1,0:T(8,128)(2,1)}, u32[]{:S(2)}) copy-start(bf16[16,2048]{1,0:T(8,128)(2,1)} %param.15) | copy-start | bytes 196612
  7.2 71.1 %all-gather.11.cloned.1.call-start = ((), (), s32[]{:S(2)}) async-start(), calls=%async_computation.12 | async-start | bytes 4718592 | tf_op jit(solution)/shard_map/all_gather | solution.py:90
  7.9 73.5 %all-gather.9.cloned.1.call-start = ((), (), s32[]{:S(2)}) async-start(), calls=%async_computation.11 | async-start | bytes 4718592 | tf_op jit(solution)/shard_map/all_gather | solution.py:89
  8.8 12.0 %copy-start.12 = (f32[16,8]{1,0:T(8,128)}, f32[16,8]{1,0:T(8,128)S(1)}, u32[]{:S(2)}) copy-start(f32[16,8]{1,0:T(8,128)S(1)} %copy.23) | copy-start | bytes 1540
  9.5 11.5 %copy-start.10 = (s32[16,8]{1,0:T(8,128)}, s32[16,8]{1,0:T(8,128)S(1)}, u32[]{:S(2)}) copy-start(s32[16,8]{1,0:T(8,128)S(1)} %multiply_add_fusion) | copy-start | bytes 1540
  9.5 11.3 %copy-start.6 = (bf16[16,2048]{1,0:T(8,128)(2,1)S(1)}, bf16[16,2048]{1,0:T(8,128)(2,1)}, u32[]{:S(2)}) copy-start(bf16[16,2048]{1,0:T(8,128)(2,1)} %param.8) | copy-start | bytes 196612
  9.7 11.9 %copy-start.8 = (bf16[16,176]{1,0:T(8,128)(2,1)}, bf16[16,176]{1,0:T(8,128)(2,1)S(1)}, u32[]{:S(2)}) copy-start(bf16[16,176]{1,0:T(8,128)(2,1)S(1)} %get-tuple-element.10) | copy-start | bytes 16900
  9.7 11.8 %copy-start.7 = (f32[2048]{0:T(1024)S(1)}, f32[2048]{0:T(1024)}, u32[]{:S(2)}) copy-start(f32[2048]{0:T(1024)} %param.9) | copy-start | bytes 24580
  11.7 35.8 %all-to-all-start.2 = ((bf16[16,11,2048]{2,1,0:T(8,128)(2,1)}), bf16[16,11,2048]{2,1,0:T(8,128)(2,1)S(1)}, u32[]{:S(2)}, u32[]{:S(2)}) async-start(bf16[16,11,2048]{2,1,0:T(8,128)(2,1)} %reshape.111), calls=%async_computation.2 | async-start | bytes 2097152 | tf_op jit(solution)/shard_map/all_to_all | solution.py:79
  20.0 64.0 %all-gather.7.cloned.1.call-start = ((), (), s32[]{:S(2)}) async-start(), calls=%async_computation.10 | async-start | bytes 4718592 | tf_op jit(solution)/shard_map/all_gather | solution.py:88
  21.5 26.0 %copy-start.14 = (f32[16]{0:T(128)}, f32[16]{0:T(128)S(1)}, u32[]{:S(2)}) copy-start(f32[16]{0:T(128)S(1)} %get-tuple-element.17) | copy-start | bytes 196
  47.5 30.5 %all-to-all-start = ((bf16[16,11,2048]{2,1,0:T(8,128)(2,1)}), bf16[16,11,2048]{2,1,0:T(8,128)(2,1)S(1)}, u32[]{:S(2)}, u32[]{:S(2)}) async-start(bf16[16,11,2048]{2,1,0:T(8,128)(2,1)} %reshape.107), calls=%async_computation | async-start | bytes 2097152 | tf_op jit(solution)/shard_map/all_to_all | solution.py:72
  51.2 139.6 %reduce-scatter.8.cloned.1.call-start = ((), (), s32[]{:S(2)}) async-start(), calls=%async_computation.9 | async-start | bytes 9437184 | tf_op jit(solution)/shard_map/reduce_scatter | solution.py:102
  86.9 3.7 %copy-start.2 = (bf16[176,768]{1,0:T(8,128)(2,1)}, bf16[176,768]{1,0:T(8,128)(2,1)S(1)}, u32[]{:S(2)}) copy-start(bf16[176,768]{1,0:T(8,128)(2,1)S(1)} %get-tuple-element.11) | copy-start | bytes 811012
  86.9 7.8 %copy-start.4 = (bf16[176,768]{1,0:T(8,128)(2,1)}, bf16[176,768]{1,0:T(8,128)(2,1)S(1)}, u32[]{:S(2)}) copy-start(bf16[176,768]{1,0:T(8,128)(2,1)S(1)} %get-tuple-element.12) | copy-start | bytes 811012
  90.5 103.6 %reduce-scatter.4.cloned.1.call-start = ((), (), s32[]{:S(2)}) async-start(), calls=%async_computation.7 | async-start | bytes 9437184 | tf_op jit(solution)/shard_map/reduce_scatter | solution.py:100
  94.6 102.7 %reduce-scatter.6.cloned.1.call-start = ((), (), s32[]{:S(2)}) async-start(), calls=%async_computation.8 | async-start | bytes 9437184 | tf_op jit(solution)/shard_map/reduce_scatter | solution.py:101
  99.5 10.7 %copy-start = (bf16[1,2048,768]{2,1,0:T(8,128)(2,1)S(1)}, bf16[1,2048,768]{2,1,0:T(8,128)(2,1)}, u32[]{:S(2)}) copy-start(bf16[1,2048,768]{2,1,0:T(8,128)(2,1)} %all-gather.9.cloned.1.call-done) | copy-start | bytes 9437188
  105.7 6.8 %copy-start.3 = (bf16[176,768]{1,0:T(8,128)(2,1)S(1)}, bf16[176,768]{1,0:T(8,128)(2,1)}, u32[]{:S(2)}) copy-start(bf16[176,768]{1,0:T(8,128)(2,1)} %copy-done.2) | copy-start | bytes 811012
  105.7 30.7 %all-to-all-start.1 = ((bf16[16,11,2048]{2,1,0:T(8,128)(2,1)}), bf16[16,11,2048]{2,1,0:T(8,128)(2,1)}, u32[]{:S(2)}, u32[]{:S(2)}) async-start(bf16[16,11,2048]{2,1,0:T(8,128)(2,1)} %reshape.109), calls=%async_computation.1 | async-start | bytes 2097152 | tf_op jit(solution)/shard_map/all_to_all | solution.py:107
  110.2 2.3 %copy-start.1 = (bf16[1,2048,768]{2,1,0:T(8,128)(2,1)S(1)}, bf16[1,2048,768]{2,1,0:T(8,128)(2,1)}, u32[]{:S(2)}) copy-start(bf16[1,2048,768]{2,1,0:T(8,128)(2,1)} %all-gather.7.cloned.1.call-done) | copy-start | bytes 9437188
  113.7 28.1 %copy-start.11 = (s32[16,8]{1,0:T(8,128)S(1)}, s32[16,8]{1,0:T(8,128)}, u32[]{:S(2)}) copy-start(s32[16,8]{1,0:T(8,128)} %copy-done.10) | copy-start | bytes 1540
  113.7 28.1 %copy-start.13 = (f32[16,8]{1,0:T(8,128)S(1)}, f32[16,8]{1,0:T(8,128)}, u32[]{:S(2)}) copy-start(f32[16,8]{1,0:T(8,128)} %copy-done.12) | copy-start | bytes 1540
  136.4 30.4 %all-to-all-start.3 = ((bf16[16,11,2048]{2,1,0:T(8,128)(2,1)}), bf16[16,11,2048]{2,1,0:T(8,128)(2,1)S(1)}, u32[]{:S(2)}, u32[]{:S(2)}) async-start(bf16[16,11,2048]{2,1,0:T(8,128)(2,1)} %reshape.113), calls=%async_computation.3 | async-start | bytes 2097152 | tf_op jit(solution)/shard_map/all_to_all | solution.py:114
  140.3 26.8 %copy-start.9 = (bf16[16,176]{1,0:T(8,128)(2,1)S(1)}, bf16[16,176]{1,0:T(8,128)(2,1)}, u32[]{:S(2)}) copy-start(bf16[16,176]{1,0:T(8,128)(2,1)} %copy-done.8) | copy-start | bytes 16900
  140.3 26.8 %copy-start.15 = (f32[16]{0:T(128)S(1)}, f32[16]{0:T(128)}, u32[]{:S(2)}) copy-start(f32[16]{0:T(128)} %copy-done.14) | copy-start | bytes 196
  141.8 48.3 %copy-start.18 = (f32[16]{0:T(128)S(1)}, f32[16]{0:T(128)}, u32[]{:S(2)}) copy-start(f32[16]{0:T(128)} %get-tuple-element.16) | copy-start | bytes 196
Sparse Core Ops, SparseCore 0:
  9.6 14.8 all-gather.10
  26.0 13.1 all-gather.8
  40.8 13.1 all-gather.6
  90.6 11.2 reduce-scatter.7
  104.1 15.8 reduce-scatter.3
  122.1 15.0 reduce-scatter.5
